TPU v7x, 128 devices: a whole 4x4x4 slice. The times are simulated.
128 devices in a mesh: row: 8 (over x_hi, z), col: 8 (over x_lo, y), layer: 2 (over core).
Axes of the slice: x: 4 (x_hi: 2, x_lo: 2; x = x_hi * 2 + x_lo), y: 4, z: 4, core: 2. Of those that a mesh axis runs over, the one named last changes fastest.
Arguments:
- matrix: float32 [32, 512, 32, 512], P('row', None, 'col', 'layer'), may hold values from -40 to 40, as said below
- transforms: float32 [1, 16, 1024, 1024], P(None, 'row', ('col', 'layer')), may hold values from -0.1875 to 0.1875
Outputs:
- swept: float32 [32, 512, 32, 512], P('row', None, 'col', 'layer')
Inputs may be any that keep to these rules, and one draw needn't show every extreme that they name: `matrix`: symmetric: entry [i, a, j, b] equals entry [j, b, i, a].
All inputs are finite; a program needn't handle non-finite values.
Results may differ from a plain program's by a relative error of at most 0.0001.
Values sent between devices are 32-bit elements; how exact they have to be, the bound alone decides.
No kernel may reach another device: no remote copies, remote signals or barrier semaphores. Data moves between devices by JAX's collectives and lax.ppermute only.
A program may use at most 192 MiB of HBM per device.

v0:
```python
import jax
import jax.numpy as jnp
from jax import lax
from jax.sharding import PartitionSpec as P

exact_mode = lax.Precision.HIGHEST


def broadcast(x, axis, root):
    mine = lax.axis_index(axis) == root
    return lax.psum(jnp.where(mine, x, jnp.zeros_like(x)), axis)


def cut_along(x, dim, count):
    before, after = (x.shape[:dim], x.shape[dim + 1 :])
    return jnp.moveaxis(x.reshape(*before, count, -1, *after), dim, 0)


def sum_at_owner(x, axis, dim):
    count = lax.axis_size(axis)
    blocks = lax.all_to_all(cut_along(x, dim, count), axis, 0, 0, tiled=True)
    return jnp.sum(blocks, axis=0)


def passed_along(block, axis, distance):
    devices = range(lax.axis_size(axis))
    route = [(i - distance, i) for i in devices if i - distance in devices]
    return lax.ppermute(block, axis, route)


def split_slots(array, axis_dim):
    return [
        lax.index_in_dim(array, index, axis_dim, keepdims=False)
        for index in range(array.shape[axis_dim])
    ]


def leading(slots):
    width = len(slots)
    return slots[width - 2]


def rearranged(slots, from_prev, from_next, position, count):
    width = len(slots)
    result = [jnp.where(position == 0, slots[0], from_prev)]
    for local in range(1, width):
        if local % 2 == 1:
            if local == width - 1:
                result.append(jnp.where(position == count - 1, slots[width - 2], from_next))
            else:
                result.append(slots[local + 2])
        else:
            result.append(jnp.where(position == 0, slots[1], slots[0]))
    return result


def shards(matrix, transforms):
    pair_dev = matrix.shape[0] // 2
    block_size = matrix.shape[1]
    half_width = matrix.shape[3]
    width = 2 * pair_dev
    pairs_row = lax.axis_size("row")
    pairs_col = lax.axis_size("col")
    row_pos = lax.axis_index("row")
    col_pos = lax.axis_index("col")
    layer_pos = lax.axis_index("layer")
    current = matrix
    left_panel = lax.all_gather(transforms[0], ("col", "layer"), axis=1, tiled=True)
    shaped = left_panel.reshape(pair_dev, 2, block_size, 2 * block_size)
    selected = lax.dynamic_slice_in_dim(shaped, layer_pos * half_width, half_width, 2)
    right_part = broadcast(selected, "row", col_pos)
    grouped = current.reshape(pair_dev, 2 * block_size, width * half_width)
    partial_rows = jnp.einsum(
        "pka,pkc->pac",
        left_panel,
        grouped,
        precision=exact_mode,
        preferred_element_type=jnp.float32,
    )
    partial_rows = partial_rows.reshape(pair_dev, 2 * block_size, pair_dev, 2, half_width)
    term_pairs = jnp.einsum(
        "paqmh,qmhb->paqb",
        partial_rows,
        right_part,
        precision=exact_mode,
        preferred_element_type=jnp.float32,
    )
    term_pairs = term_pairs.reshape(pair_dev, 2 * block_size, pair_dev, 2, 2, half_width)
    rotated = sum_at_owner(term_pairs, "layer", 4)
    rotated = rotated.reshape(width, block_size, width, half_width)
    rows = split_slots(rotated, 0)
    upward = passed_along(leading(rows), "row", 1)
    downward = passed_along(rows[1], "row", -1)
    moved = jnp.stack(rearranged(rows, upward, downward, row_pos, pairs_row), 0)
    cols = split_slots(moved, 2)
    upward_cols = passed_along(leading(cols), "col", 1)
    downward_cols = passed_along(cols[1], "col", -1)
    current = jnp.stack(rearranged(cols, upward_cols, downward_cols, col_pos, pairs_col), 2)
    return current


def solution(mesh):
    return jax.shard_map(
        shards,
        mesh=mesh,
        in_specs=(P("row", None, "col", "layer"), P(None, "row", ("col", "layer"), None)),
        out_specs=P("row", None, "col", "layer"),
        check_vma=False,
    )
```

profile of v0, /device:TPU:120, one launch (start us, length us, event | category | flops | bytes accessed | tf_op | source)
XLA Modules:
  0.0 413.2 jit_solution(15162404626442989335)
XLA Ops:
  7.3 54.8 %all-gather.3.cloned.1.call-done = f32[1,2,1024,1024]{3,2,1,0:T(8,128)} async-done(((f32[1,2,64,1024]{3,2,1,0:T(8,128)}), f32[1,2,1024,1024]{3,2,1,0:T(8,128)}) %all-gather.3.cloned.1.call-update) | async-done | bytes 8388624 | tf_op jit(solution)/shard_map/all_gather | solution.py:68
  62.1 4.8 %constant_dynamic-slice_fusion = f32[2,2,256,1024]{3,2,1,0:T(8,128)} fusion(f32[2,2,512,1024]{3,2,1,0:T(8,128)} %bitcast.73, s32[]{:T(128)S(6)} %select_n.56), kind=kLoop, calls=%fused_computation.23 | loop fusion | bytes 8388612 | tf_op jit(solution)/shard_map/dynamic_slice | solution.py:70
  66.9 5.4 %copy.45 = f32[2,2,256,1024]{2,3,1,0:T(8,128)} copy(f32[2,2,256,1024]{3,2,1,0:T(8,128)} %constant_dynamic-slice_fusion) | data formatting | bytes 8388608
  72.3 4.5 %broadcast_select_fusion = f32[2,2,256,1024]{2,3,1,0:T(8,128)} fusion(f32[2,2,256,1024]{2,3,1,0:T(8,128)} %copy.45, pred[]{:T(512)S(6)} %eq.19), kind=kLoop, calls=%fused_computation.20 | loop fusion | flops 1048576 | bytes 8388609 | tf_op jit(solution)/shard_map/jit(_where)/select_n | solution.py:11
  76.9 10.7 %reshape.15 = f32[2,1024,1024]{2,1,0:T(8,128)} reshape(f32[4,512,4,256]{3,2,1,0:T(4,128)} %param.2) | data formatting | bytes 16777216 | tf_op jit(solution)/shard_map/reshape | solution.py:72
  87.6 31.5 %fusion.2 = f32[2,1024,1024]{1,2,0:T(8,128)} fusion(f32[2,1024,1024]{2,1,0:T(8,128)} %reshape.15, f32[1,2,1024,1024]{3,2,1,0:T(8,128)} %all-gather.3.cloned.1.call-done), kind=kOutput, calls=%fused_computation.5 | convolution fusion | flops 25769803776 | bytes 25165824 | tf_op jit(solution)/shard_map/pka,pkc->pac/dot_general | solution.py:73
  119.1 66.1 %all-reduce.2.cloned.1.call-done = f32[2,2,256,1024]{2,3,1,0:T(8,128)} async-done(((f32[2,2,256,1024]{2,3,1,0:T(8,128)}), f32[2,2,256,1024]{2,3,1,0:T(8,128)}) %all-reduce.2.cloned.1.call-update) | async-done | bytes 4194320 | tf_op jit(solution)/shard_map/psum | solution.py:11
  185.2 31.1 %fusion = f32[2,1024,2,1024,1]{3,1,4,2,0:T(8,128)S(1)} fusion(f32[2,1024,2,2,256]{1,4,3,2,0:T(8,128)} %bitcast.72, f32[2,2,256,1024]{2,3,1,0:T(8,128)} %all-reduce.2.cloned.1.call-done), kind=kOutput, calls=%fused_computation.3 | convolution fusion | flops 25769803776 | bytes 29360128 | tf_op jit(solution)/shard_map/paqmh,qmhb->paqb/dot_general | solution.py:81
  216.3 2.9 copy.55
  219.2 19.0 %all_to_all.5 = f32[2,2,1024,2,2,1,256]{2,6,4,1,3,5,0:T(8,128)} all-to-all(f32[2,2,1024,2,2,1,256]{2,6,4,1,3,5,0:T(8,128)S(1)} %bitcast.68), channel_id=1, replica_groups=mesh['row'=8,'col'=8,'layer'=2] {'layer'}, dimensions={0} | all-to-all | bytes 33554432 | tf_op jit(solution)/shard_map/all_to_all | solution.py:21
  238.3 12.2 %reduce_sum.9 = f32[2,1024,2,2,256]{1,4,3,0,2:T(8,128)} reduce(f32[2,2,1024,2,2,1,256]{2,6,4,1,3,5,0:T(8,128)} %all_to_all.5, f32[]{:T(128)} %constant.21.clone.1), dimensions={0,5}, to_apply=%region_1.2 | reduce | flops 2097152 | bytes 25165828 | tf_op jit(solution)/shard_map/reduce_sum | solution.py:22
  250.5 8.7 %copy.29 = f32[2,1024,2,2,256]{4,1,0,3,2:T(8,128)} copy(f32[2,1024,2,2,256]{1,4,3,0,2:T(8,128)} %reduce_sum.9) | data formatting | bytes 16777216 | tf_op jit(solution)/shard_map/reduce_sum | solution.py:22
  259.2 5.4 %slice_bitcast_fusion.3 = (f32[512,4,256]{2,0,1:T(8,128)}, f32[512,4,256]{2,0,1:T(8,128)}, f32[1,512,4,256]{3,1,2,0:T(8,128)S(1)}) fusion(f32[4,512,4,256]{3,1,0,2:T(8,128)} %bitcast.69), kind=kLoop, calls=%fused_computation.11 | loop fusion | bytes 12582912 | tf_op jit(solution)/shard_map/squeeze | solution.py:33
  264.6 4.7 %collective-permute-start = (f32[512,4,256]{2,0,1:T(8,128)}, f32[512,4,256]{2,0,1:T(8,128)}, u32[]{:S(2)}, u32[]{:S(2)}) collective-permute-start(f32[512,4,256]{2,0,1:T(8,128)} %get-tuple-element.12), channel_id=1, source_target_pairs={{0,16},{16,32},{32,48},{48,64},{64,80},{80,96},{96,112},{1,17},{17... | collective-permute-start | bytes 6291464 | tf_op jit(solution)/shard_map/ppermute | solution.py:28
  273.7 41.0 %collective-permute-done = f32[512,4,256]{2,0,1:T(8,128)} collective-permute-done((f32[512,4,256]{2,0,1:T(8,128)}, f32[512,4,256]{2,0,1:T(8,128)}, u32[]{:S(2)}, u32[]{:S(2)}) %collective-permute-start) | collective-permute-done | bytes 2097184 | tf_op jit(solution)/shard_map/ppermute | solution.py:28
  314.8 7.7 %collective-permute-done.1 = f32[512,4,256]{2,0,1:T(8,128)} collective-permute-done((f32[512,4,256]{2,0,1:T(8,128)}, f32[512,4,256]{2,0,1:T(8,128)}, u32[]{:S(2)}, u32[]{:S(2)}) %collective-permute-start.1) | collective-permute-done | bytes 2097184 | tf_op jit(solution)/shard_map/ppermute | solution.py:28
  322.5 4.2 %fusion.6 = (f32[1,512,4,256]{3,1,2,0:T(8,128)S(1)}, f32[1,512,4,256]{3,1,2,0:T(8,128)S(1)}) fusion(f32[512,4,256]{2,0,1:T(8,128)} %collective-permute-done, f32[4,512,4,256]{3,1,0,2:T(8,128)} %bitcast.71, pred[]{:T(512)S(6)} %eq.18, f32[512,4,256]{2,0,1:T(8,128)} %collective-permute-done.1, pred[]{:T(512)S(6)} %eq.20), kind=kLoop, calls=%fused_computation.16 | loop fusion | flops 1048576 | bytes 12582914 | tf_op jit(solution)/shard_map/stack | solution.py:94
  327.8 3.0 slice_bitcast_fusion.1
  332.4 3.3 collective-permute-start.2
  340.8 40.3 %collective-permute-done.2 = f32[4,512,256]{2,1,0:T(8,128)} collective-permute-done((f32[4,512,256]{2,1,0:T(8,128)}, f32[4,512,256]{2,1,0:T(8,128)}, u32[]{:S(2)}, u32[]{:S(2)}) %collective-permute-start.2) | collective-permute-done | bytes 2097184 | tf_op jit(solution)/shard_map/ppermute | solution.py:28
  381.1 5.1 %collective-permute-done.3 = f32[4,512,256]{2,1,0:T(8,128)} collective-permute-done((f32[4,512,256]{2,1,0:T(8,128)}, f32[4,512,256]{2,1,0:T(8,128)}, u32[]{:S(2)}, u32[]{:S(2)}) %collective-permute-start.3) | collective-permute-done | bytes 2097184 | tf_op jit(solution)/shard_map/ppermute | solution.py:28
  386.3 4.2 %fusion.5 = (f32[4,512,1,256]{3,1,0,2:T(8,128)S(1)}, f32[4,512,1,256]{3,1,0,2:T(8,128)S(1)}) fusion(f32[4,512,256]{2,1,0:T(8,128)} %collective-permute-done.2, f32[4,512,4,256]{3,1,2,0:T(8,128)} %copy-done, pred[]{:T(512)S(6)} %eq.17, f32[4,512,256]{2,1,0:T(8,128)} %collective-permute-done.3, pred[]{:T(512)S(6)} %eq.21), kind=kLoop, calls=%fused_computation.13 | loop fusion | flops 1048576 | bytes 12582914 | tf_op jit(solution)/shard_map/stack | solution.py:98
  390.5 3.7 pad_maximum_fusion.1
  394.2 12.2 %copy.38 = f32[4,512,4,256]{3,2,1,0:T(4,128)} copy(f32[4,512,4,256]{3,1,0,2:T(8,128)} %pad_maximum_fusion.1) | data formatting | bytes 16777216 | tf_op jit(solution)/shard_map/stack | solution.py:98
  (11 shorter events, 12.9 us)
Async XLA Ops:
  6.5 55.6 %all-gather.3.cloned.1.call-start = ((), (), s32[]{:S(2)}) async-start(), calls=%async_computation.2 | async-start | bytes 8912896 | tf_op jit(solution)/shard_map/all_gather | solution.py:68
  7.3 177.9 %all-reduce.2.cloned.1.call-start = ((), (), s32[]{:S(2)}) async-start(), calls=%async_computation.1 | async-start | bytes 8388608 | tf_op jit(solution)/shard_map/psum | solution.py:11
  264.6 50.2 %collective-permute-start = (f32[512,4,256]{2,0,1:T(8,128)}, f32[512,4,256]{2,0,1:T(8,128)}, u32[]{:S(2)}, u32[]{:S(2)}) collective-permute-start(f32[512,4,256]{2,0,1:T(8,128)} %get-tuple-element.12), channel_id=1, source_target_pairs={{0,16},{16,32},{32,48},{48,64},{64,80},{80,96},{96,112},{1,17},{17... | collective-permute-start | bytes 6291464 | tf_op jit(solution)/shard_map/ppermute | solution.py:28
  269.3 53.2 %collective-permute-start.1 = (f32[512,4,256]{2,0,1:T(8,128)}, f32[512,4,256]{2,0,1:T(8,128)}, u32[]{:S(2)}, u32[]{:S(2)}) collective-permute-start(f32[512,4,256]{2,0,1:T(8,128)} %get-tuple-element.13), channel_id=1, source_target_pairs={{16,0},{32,16},{48,32},{64,48},{80,64},{96,80},{112,96},{17,1},{33... | collective-permute-start | bytes 6291464 | tf_op jit(solution)/shard_map/ppermute | solution.py:28
  327.7 4.7 %copy-start = (f32[4,512,4,256]{3,1,2,0:T(8,128)}, f32[4,512,4,256]{3,1,2,0:T(8,128)S(1)}, u32[]{:S(2)}) copy-start(f32[4,512,4,256]{3,1,2,0:T(8,128)S(1)} %pad_maximum_fusion) | copy-start | bytes 25165828
  332.4 48.7 %collective-permute-start.2 = (f32[4,512,256]{2,1,0:T(8,128)}, f32[4,512,256]{2,1,0:T(8,128)}, u32[]{:S(2)}, u32[]{:S(2)}) collective-permute-start(f32[4,512,256]{2,1,0:T(8,128)} %get-tuple-element.7), channel_id=1, source_target_pairs={{0,2},{2,4},{4,6},{6,8},{8,10},{10,12},{12,14},{1,3},{3,5},{5,7},{... | collective-permute-start | bytes 6291464 | tf_op jit(solution)/shard_map/ppermute | solution.py:28
  335.7 50.6 %collective-permute-start.3 = (f32[4,512,256]{2,1,0:T(8,128)}, f32[4,512,256]{2,1,0:T(8,128)}, u32[]{:S(2)}, u32[]{:S(2)}) collective-permute-start(f32[4,512,256]{2,1,0:T(8,128)} %get-tuple-element.8), channel_id=1, source_target_pairs={{2,0},{4,2},{6,4},{8,6},{10,8},{12,10},{14,12},{3,1},{5,3},{7,5},{... | collective-permute-start | bytes 6291464 | tf_op jit(solution)/shard_map/ppermute | solution.py:28
Sparse Core Ops, SparseCore 0:
  9.0 53.0 all-gather.2
  77.0 108.1 all-reduce.1
where the time goes:
time: 414 us; the launch traced here: 413 us
  waiting for transfers between devices  216 us (52%)
  matrix products  62.6 us (15%)
  local copies, waits for them, and re-layouts  54.7 us (13%)
  other arithmetic  34.9 us (8%)
  blocking collectives  19 us (5%)
  between operations  13.5 us (3%)
  starting transfers between devices  12.5 us (3%)
    ppermute x4, waiting for transfers between devices, passed_along(): return lax.ppermute(block, axis, route)  94.2 us
    psum x1, waiting for transfers between devices, broadcast(): return lax.psum(jnp.where(mine, x, jnp.zeros_like(x)), axis)  66.1 us
    all_gather x1, waiting for transfers between devices, shards(): lax.all_gather(transforms[0], ('col', 'layer'), axis=1, tiled=True)  54.8 us
    dot_general x1, matrix products, shards(): jnp.einsum('pka,pkc->pac', left_panel, grouped, precision=exact_mode, pre...  31.5 us
    dot_general x1, matrix products, shards(): jnp.einsum('paqmh,qmhb->paqb', partial_rows, right_part, precision=exact_...  31.1 us
    all_to_all x1, blocking collectives, sum_at_owner(): blocks = lax.all_to_all(cut_along(x, dim, count), axis, 0, 0, tiled=True)  19 us
    ppermute x4, starting transfers between devices, passed_along(): return lax.ppermute(block, axis, route)  12.5 us
    reduce_sum x1, other arithmetic, sum_at_owner(): return jnp.sum(blocks, axis=0)  12.2 us
  transfers between devices with their start and end apart: 6, of which 6 were waited for; matrix products, arithmetic and copies ran while one was open for 11% of the time, Pallas kernels for 0%

commit v1 on v0

--- a/solution.py
+++ b/solution.py
@@ -65,7 +65,12 @@
     col_pos = lax.axis_index("col")
     layer_pos = lax.axis_index("layer")
     current = matrix
-    left_panel = lax.all_gather(transforms[0], ("col", "layer"), axis=1, tiled=True)
+    left_panel = jnp.concatenate(
+        lax.all_to_all(
+            jnp.stack([transforms[0]] * lax.axis_size(("col", "layer"))), ("col", "layer"), 0, 0
+        ),
+        axis=1,
+    )
     shaped = left_panel.reshape(pair_dev, 2, block_size, 2 * block_size)
     selected = lax.dynamic_slice_in_dim(shaped, layer_pos * half_width, half_width, 2)
     right_part = broadcast(selected, "row", col_pos)

time: 414 us -> 503 us (1.21)
  waiting for transfers between devices: 216 us -> 288 us
  local copies, waits for them, and re-layouts: 54.7 us -> 65.3 us
  starting transfers between devices: 12.5 us -> 18.1 us
    all_to_all x0 -> x1, waiting for transfers between devices: none -> 128 us  [shards(): lax.all_to_all(jnp.stack([transforms[0]] * lax.axis_size(('col', 'layer')...]
    all_gather x1 -> x0, waiting for transfers between devices: 54.8 us -> none  [shards(): lax.all_gather(transforms[0], ('col', 'layer'), axis=1, tiled=True)]
    all_to_all x0 -> x1, starting transfers between devices: none -> 5.63 us  [shards(): lax.all_to_all(jnp.stack([transforms[0]] * lax.axis_size(('col', 'layer')...]
    another operation x0 -> x1, local copies, waits for them, and re-layouts: none -> 5.5 us  [shards(): jnp.stack([transforms[0]] * lax.axis_size(('col', 'layer')))]
    unnamed x3 -> x5, local copies, waits for them, and re-layouts: 6.99 us -> 10.4 us
  transfers between devices with their start and end apart: 6 -> 6, of which waited for: 6 -> 6; matrix products, arithmetic and copies ran while one was open for 11% -> 9% of each run, Pallas kernels for 0% -> 0%
where the time goes in v1:
time: 503 us; the launch traced here: 502 us
  waiting for transfers between devices  288 us (57%)
  local copies, waits for them, and re-layouts  65.3 us (13%)
  matrix products  62.6 us (12%)
  other arithmetic  34.9 us (7%)
  blocking collectives  19 us (4%)
  starting transfers between devices  18.1 us (4%)
  between operations  13.5 us (3%)
    all_to_all x1, waiting for transfers between devices, shards(): lax.all_to_all(jnp.stack([transforms[0]] * lax.axis_size(('col', 'layer')...  128 us
    ppermute x4, waiting for transfers between devices, passed_along(): return lax.ppermute(block, axis, route)  94.2 us
    psum x1, waiting for transfers between devices, broadcast(): return lax.psum(jnp.where(mine, x, jnp.zeros_like(x)), axis)  65.7 us
    dot_general x1, matrix products, shards(): jnp.einsum('pka,pkc->pac', left_panel, grouped, precision=exact_mode, pre...  31.5 us
    dot_general x1, matrix products, shards(): jnp.einsum('paqmh,qmhb->paqb', partial_rows, right_part, precision=exact_...  31.1 us
    all_to_all x1, blocking collectives, sum_at_owner(): blocks = lax.all_to_all(cut_along(x, dim, count), axis, 0, 0, tiled=True)  19 us
    ppermute x4, starting transfers between devices, passed_along(): return lax.ppermute(block, axis, route)  12.5 us
    reduce_sum x1, other arithmetic, sum_at_owner(): return jnp.sum(blocks, axis=0)  12.2 us
  transfers between devices with their start and end apart: 6, of which 6 were waited for; matrix products, arithmetic and copies ran while one was open for 9% of the time, Pallas kernels for 0%

profile of v1, /device:TPU:120, one launch (start us, length us, event | category | flops | bytes accessed | tf_op | source)
XLA Modules:
  0.0 501.7 jit_solution(2771019786056694332)
XLA Ops:
  6.5 5.5 %stack.23 = f32[16,2,64,1024]{3,2,1,0:T(8,128)} broadcast(f32[2,64,1024]{2,1,0:T(8,128)} %bitcast.78), dimensions={1,2,3} | broadcast | bytes 8912896 | tf_op jit(solution)/shard_map/stack | solution.py:70
  12.0 5.6 %all-to-all-start = ((f32[16,2,64,1024]{3,2,1,0:T(8,128)}), f32[16,2,64,1024]{3,2,1,0:T(8,128)}, u32[]{:S(2)}, u32[]{:S(2)}) async-start(f32[16,2,64,1024]{3,2,1,0:T(8,128)} %stack.23), calls=%async_computation | async-start | bytes 16777216 | tf_op jit(solution)/shard_map/all_to_all | solution.py:69
  17.7 128.2 %all-to-all-done = f32[16,2,64,1024]{3,2,1,0:T(8,128)} async-done(((f32[16,2,64,1024]{3,2,1,0:T(8,128)}), f32[16,2,64,1024]{3,2,1,0:T(8,128)}, u32[]{:S(2)}, u32[]{:S(2)}) %all-to-all-start) | async-done | bytes 8388640 | tf_op jit(solution)/shard_map/all_to_all | solution.py:69
  145.9 4.2 copy.23
  150.2 3.4 copy-done.1
  155.8 5.4 %copy.45 = f32[2,2,256,1024]{2,3,1,0:T(8,128)} copy(f32[2,2,256,1024]{3,2,1,0:T(8,128)} %constant_dynamic-slice_fusion) | data formatting | bytes 8388608
  161.2 4.5 broadcast_select_fusion
  165.8 10.7 %reshape.20 = f32[2,1024,1024]{2,1,0:T(8,128)} reshape(f32[4,512,4,256]{3,2,1,0:T(4,128)} %param.2) | data formatting | bytes 16777216 | tf_op jit(solution)/shard_map/reshape | solution.py:77
  176.5 31.5 %fusion.5 = f32[2,1024,1024]{1,2,0:T(8,128)} fusion(f32[2,1024,1024]{2,1,0:T(8,128)} %bitcast.76, f32[2,1024,1024]{2,1,0:T(8,128)} %reshape.20), kind=kOutput, calls=%fused_computation.22 | convolution fusion | flops 25769803776 | bytes 25165824 | tf_op jit(solution)/shard_map/pka,pkc->pac/dot_general | solution.py:78
  208.0 65.7 %all-reduce.2.cloned.1.call-done = f32[2,2,256,1024]{2,3,1,0:T(8,128)} async-done(((f32[2,2,256,1024]{2,3,1,0:T(8,128)}), f32[2,2,256,1024]{2,3,1,0:T(8,128)}) %all-reduce.2.cloned.1.call-update) | async-done | bytes 4194320 | tf_op jit(solution)/shard_map/psum | solution.py:11
  273.7 31.1 %fusion = f32[2,1024,2,1024,1]{3,1,4,2,0:T(8,128)S(1)} fusion(f32[2,1024,2,2,256]{1,4,3,2,0:T(8,128)} %bitcast.77, f32[2,2,256,1024]{2,3,1,0:T(8,128)} %all-reduce.2.cloned.1.call-done), kind=kOutput, calls=%fused_computation.3 | convolution fusion | flops 25769803776 | bytes 29360128 | tf_op jit(solution)/shard_map/paqmh,qmhb->paqb/dot_general | solution.py:86
  307.7 19.0 %all_to_all.10 = f32[2,2,1024,2,2,1,256]{2,6,4,1,3,5,0:T(8,128)} all-to-all(f32[2,2,1024,2,2,1,256]{2,6,4,1,3,5,0:T(8,128)S(1)} %bitcast.71), channel_id=1, replica_groups=mesh['row'=8,'col'=8,'layer'=2] {'layer'}, dimensions={0} | all-to-all | bytes 33554432 | tf_op jit(solution)/shard_map/all_to_all | solution.py:21
  326.8 12.2 %reduce_sum.9 = f32[2,1024,2,2,256]{1,4,3,0,2:T(8,128)} reduce(f32[2,2,1024,2,2,1,256]{2,6,4,1,3,5,0:T(8,128)} %all_to_all.10, f32[]{:T(128)} %constant.21.clone.1), dimensions={0,5}, to_apply=%region_1.2 | reduce | flops 2097152 | bytes 25165828 | tf_op jit(solution)/shard_map/reduce_sum | solution.py:22
  339.0 8.7 %copy.29 = f32[2,1024,2,2,256]{4,1,0,3,2:T(8,128)} copy(f32[2,1024,2,2,256]{1,4,3,0,2:T(8,128)} %reduce_sum.9) | data formatting | bytes 16777216 | tf_op jit(solution)/shard_map/reduce_sum | solution.py:22
  347.7 5.4 %slice_bitcast_fusion.3 = (f32[512,4,256]{2,0,1:T(8,128)}, f32[512,4,256]{2,0,1:T(8,128)}, f32[1,512,4,256]{3,1,2,0:T(8,128)S(1)}) fusion(f32[4,512,4,256]{3,1,0,2:T(8,128)} %bitcast.72), kind=kLoop, calls=%fused_computation.9 | loop fusion | bytes 12582912 | tf_op jit(solution)/shard_map/squeeze | solution.py:33
  353.1 4.7 collective-permute-start
  362.3 41.0 %collective-permute-done = f32[512,4,256]{2,0,1:T(8,128)} collective-permute-done((f32[512,4,256]{2,0,1:T(8,128)}, f32[512,4,256]{2,0,1:T(8,128)}, u32[]{:S(2)}, u32[]{:S(2)}) %collective-permute-start) | collective-permute-done | bytes 2097184 | tf_op jit(solution)/shard_map/ppermute | solution.py:28
  403.3 7.7 %collective-permute-done.1 = f32[512,4,256]{2,0,1:T(8,128)} collective-permute-done((f32[512,4,256]{2,0,1:T(8,128)}, f32[512,4,256]{2,0,1:T(8,128)}, u32[]{:S(2)}, u32[]{:S(2)}) %collective-permute-start.1) | collective-permute-done | bytes 2097184 | tf_op jit(solution)/shard_map/ppermute | solution.py:28
  411.0 4.2 fusion.4
  429.3 40.3 %collective-permute-done.2 = f32[4,512,256]{2,1,0:T(8,128)} collective-permute-done((f32[4,512,256]{2,1,0:T(8,128)}, f32[4,512,256]{2,1,0:T(8,128)}, u32[]{:S(2)}, u32[]{:S(2)}) %collective-permute-start.2) | collective-permute-done | bytes 2097184 | tf_op jit(solution)/shard_map/ppermute | solution.py:28
  469.6 5.1 %collective-permute-done.3 = f32[4,512,256]{2,1,0:T(8,128)} collective-permute-done((f32[4,512,256]{2,1,0:T(8,128)}, f32[4,512,256]{2,1,0:T(8,128)}, u32[]{:S(2)}, u32[]{:S(2)}) %collective-permute-start.3) | collective-permute-done | bytes 2097184 | tf_op jit(solution)/shard_map/ppermute | solution.py:28
  474.8 4.2 fusion.3
  479.0 3.7 pad_maximum_fusion.1
  482.7 12.2 %copy.38 = f32[4,512,4,256]{3,2,1,0:T(4,128)} copy(f32[4,512,4,256]{3,1,0,2:T(8,128)} %pad_maximum_fusion.1) | data formatting | bytes 16777216 | tf_op jit(solution)/shard_map/stack | solution.py:103
  (14 shorter events, 23.7 us)
Async XLA Ops:
  12.0 133.9 %all-to-all-start = ((f32[16,2,64,1024]{3,2,1,0:T(8,128)}), f32[16,2,64,1024]{3,2,1,0:T(8,128)}, u32[]{:S(2)}, u32[]{:S(2)}) async-start(f32[16,2,64,1024]{3,2,1,0:T(8,128)} %stack.23), calls=%async_computation | async-start | bytes 16777216 | tf_op jit(solution)/shard_map/all_to_all | solution.py:69
  17.7 256.0 %all-reduce.2.cloned.1.call-start = ((), (), s32[]{:S(2)}) async-start(), calls=%async_computation.2 | async-start | bytes 8388608 | tf_op jit(solution)/shard_map/psum | solution.py:11
  150.2 3.4 copy-start.1
  353.1 50.2 %collective-permute-start = (f32[512,4,256]{2,0,1:T(8,128)}, f32[512,4,256]{2,0,1:T(8,128)}, u32[]{:S(2)}, u32[]{:S(2)}) collective-permute-start(f32[512,4,256]{2,0,1:T(8,128)} %get-tuple-element.12), channel_id=1, source_target_pairs={{0,16},{16,32},{32,48},{48,64},{64,80},{80,96},{96,112},{1,17},{17... | collective-permute-start | bytes 6291464 | tf_op jit(solution)/shard_map/ppermute | solution.py:28
  357.8 53.2 %collective-permute-start.1 = (f32[512,4,256]{2,0,1:T(8,128)}, f32[512,4,256]{2,0,1:T(8,128)}, u32[]{:S(2)}, u32[]{:S(2)}) collective-permute-start(f32[512,4,256]{2,0,1:T(8,128)} %get-tuple-element.13), channel_id=1, source_target_pairs={{16,0},{32,16},{48,32},{64,48},{80,64},{96,80},{112,96},{17,1},{33... | collective-permute-start | bytes 6291464 | tf_op jit(solution)/shard_map/ppermute | solution.py:28
  416.3 4.7 copy-start
  420.9 48.7 %collective-permute-start.2 = (f32[4,512,256]{2,1,0:T(8,128)}, f32[4,512,256]{2,1,0:T(8,128)}, u32[]{:S(2)}, u32[]{:S(2)}) collective-permute-start(f32[4,512,256]{2,1,0:T(8,128)} %get-tuple-element.7), channel_id=1, source_target_pairs={{0,2},{2,4},{4,6},{6,8},{8,10},{10,12},{12,14},{1,3},{3,5},{5,7},{... | collective-permute-start | bytes 6291464 | tf_op jit(solution)/shard_map/ppermute | solution.py:28
  424.2 50.6 %collective-permute-start.3 = (f32[4,512,256]{2,1,0:T(8,128)}, f32[4,512,256]{2,1,0:T(8,128)}, u32[]{:S(2)}, u32[]{:S(2)}) collective-permute-start(f32[4,512,256]{2,1,0:T(8,128)} %get-tuple-element.8), channel_id=1, source_target_pairs={{2,0},{4,2},{6,4},{8,6},{10,8},{12,10},{14,12},{3,1},{5,3},{7,5},{... | collective-permute-start | bytes 6291464 | tf_op jit(solution)/shard_map/ppermute | solution.py:28
Sparse Core Ops, SparseCore 0:
  165.9 107.7 all-reduce.1
